TPU v7x, 256 devices: a whole 4x4x8 slice. The times are simulated.
256 devices in a mesh: row: 16 (over z, core), col: 8 (over y_hi, x), depth: 2 (over y_lo).
Axes of the slice: x: 4, y: 4 (y_hi: 2, y_lo: 2; y = y_hi * 2 + y_lo), z: 8, core: 2. Of those that a mesh axis runs over, the one named last changes fastest.
Arguments:
- a_blocks: float32 [32, 32, 256, 256], P('row', ('depth', 'col')), may hold values from -6 to 6
- a_pattern: int32 [32, 32], P('row', ('depth', 'col')), may hold values from 0 to 1, as said below
- b_blocks: float32 [32, 32, 256, 256], P(('depth', 'row'), 'col'), may hold values from -0.125 to 0.125
- b_pattern: int32 [32, 32], P(('depth', 'row'), 'col'), may hold values from 0 to 1, as said below
- c_pattern: int32 [32, 32], P(('row', 'depth'), 'col'), may hold values 0 or 1
Outputs:
- c_blocks: float32 [32, 32, 256, 256], P(('row', 'depth'), 'col')
Inputs may be any that keep to these rules, and one draw needn't show every extreme that they name: Each block row of a_pattern holds between 1 and 8 stored blocks, and some block row holds exactly 8. Each block column of b_pattern holds between 1 and 8 stored blocks, and some block column holds exactly 8.
All inputs are finite; a program needn't handle non-finite values. No bound on the sum of `c_pattern` on one device may be relied on, other than what follows from the above.
Results may differ from a plain program's by a relative error of at most 0.000071.
Values sent between devices are 32-bit elements; how exact they have to be, the bound alone decides.
A program may use at most 128 MiB of HBM per device.

v0:
```python
import jax
import jax.numpy as jnp
from jax import lax
from jax.sharding import PartitionSpec as P


def local(a_blocks, a_pattern, b_blocks, b_pattern, c_pattern):
    left = a_blocks * a_pattern[:, :, None, None].astype(jnp.float32)
    right = b_blocks * b_pattern[:, :, None, None].astype(jnp.float32)
    layer_right = lax.all_gather(right, "row", axis=0, tiled=True)
    partial_value = jnp.einsum(
        "rkab,kcbe->rcae",
        lax.all_gather(left, "col", axis=1, tiled=True),
        layer_right,
        precision=lax.Precision.HIGHEST,
    )
    product = lax.psum_scatter(partial_value, "depth", scatter_dimension=0, tiled=True)
    return product * c_pattern[:, :, None, None].astype(jnp.float32)


def solution(mesh):
    in_specs = (
        P("row", ("depth", "col"), None, None),
        P("row", ("depth", "col")),
        P(("depth", "row"), "col", None, None),
        P(("depth", "row"), "col"),
        P(("row", "depth"), "col"),
    )
    out_specs = P(("row", "depth"), "col", None, None)
    return jax.shard_map(local, mesh=mesh, in_specs=in_specs, out_specs=out_specs, check_vma=False)
```

profile of v0, /device:TPU:1, one launch (start us, length us, event | category | flops | bytes accessed | tf_op | source)
XLA Modules:
  0.0 337.4 jit_solution(12604116690690265737)
XLA Ops:
  6.5 0.0 all-gather.5.cloned.1.call-start
  6.5 0.7 convert_element_type.28
  7.2 2.3 broadcast_multiply_fusion
  9.6 0.0 all-gather.5.cloned.1.call-update
  9.6 0.0 all-gather.3.cloned.1.call-start
  9.6 1.6 copy.8
  11.2 0.7 convert_bitcast_fusion.1
  11.9 1.2 broadcast_multiply_fusion.1
  13.1 0.0 all-gather.3.cloned.1.call-update
  13.1 0.0 copy-start.1
  13.1 0.0 copy-start
  13.1 0.0 all-reduce.3.cloned.1.call-start
  13.2 114.2 %all-gather.5.cloned.1.call-done = f32[2,16,256,256]{3,2,1,0:T(8,128)} async-done(((f32[2,2,256,256]{3,2,1,0:T(8,128)}), f32[2,16,256,256]{3,2,1,0:T(8,128)}) %all-gather.5.cloned.1.call-update) | async-done | bytes 8388624 | tf_op jit(solution)/shard_map/all_gather | solution.py:13
  127.4 96.1 %all-gather.3.cloned.1.call-done = f32[16,4,256,256]{2,3,0,1:T(8,128)} async-done(((f32[1,4,256,256]{2,3,0,1:T(8,128)}), f32[16,4,256,256]{2,3,0,1:T(8,128)}) %all-gather.3.cloned.1.call-update) | async-done | bytes 16777232 | tf_op jit(solution)/shard_map/all_gather | solution.py:10
  223.5 31.1 %fusion.3 = f32[2,4,256,256]{2,3,0,1:T(8,128)} fusion(f32[2,16,256,256]{3,2,1,0:T(8,128)} %all-gather.5.cloned.1.call-done, f32[16,4,256,256]{2,3,0,1:T(8,128)} %all-gather.3.cloned.1.call-done), kind=kOutput, calls=%fused_computation.3 | convolution fusion | flops 25769803776 | bytes 27262976 | tf_op jit(solution)/shard_map/rkab,kcbe->rcae/dot_general | solution.py:11
  254.6 0.0 all-reduce.3.cloned.1.call-update
  254.6 0.0 copy-done.1
  254.6 0.6 dynamic-slice
  255.2 0.0 copy-done
  255.2 72.3 %all-reduce.3.cloned.1.call-done = f32[2,4,256,256]{2,3,0,1:T(8,128)} async-done(((f32[2,4,256,256]{2,3,0,1:T(8,128)}), f32[2,4,256,256]{2,3,0,1:T(8,128)}) %all-reduce.3.cloned.1.call-update) | async-done | bytes 2097168
  327.6 2.0 dynamic-slice_multiply_fusion
  329.6 1.3 copy.9
  (1 shorter events, 0.0 us)
Async XLA Ops:
  6.5 120.8 %all-gather.5.cloned.1.call-start = ((), (), s32[]{:S(2)}) async-start(), calls=%async_computation.1 | async-start | bytes 9437184 | tf_op jit(solution)/shard_map/all_gather | solution.py:13
  9.6 213.9 %all-gather.3.cloned.1.call-start = ((), (), s32[]{:S(2)}) async-start(), calls=%async_computation | async-start | bytes 17825792 | tf_op jit(solution)/shard_map/all_gather | solution.py:10
  13.1 241.5 %copy-start.1 = (u32[256]{0:T(256)S(1)}, u32[256]{0:T(256)}, u32[]{:S(2)}) copy-start(u32[256]{0:T(256)} %constant.7) | copy-start | bytes 3076
  13.1 242.1 %copy-start = (s32[1,4]{1,0:T(1,128)S(1)}, s32[1,4]{1,0:T(1,128)}, u32[]{:S(2)}) copy-start(s32[1,4]{1,0:T(1,128)} %param.9) | copy-start | bytes 52
  13.1 314.4 %all-reduce.3.cloned.1.call-start = ((), (), s32[]{:S(2)}) async-start(), calls=%async_computation.2 | async-start | bytes 4194304
Sparse Core Ops, SparseCore 0:
  10.0 117.3 all-gather.4
  129.2 94.1 all-gather.2
  254.7 72.7 all-reduce.2
where the time goes:
time: 338 us; the launch traced here: 337 us
  waiting for transfers between devices  283 us (84%)
  matrix products  31.1 us (9%)
  between operations  13.2 us (4%)
  other arithmetic  6.93 us (2%)
  local copies, waits for them, and re-layouts  3.46 us (1%)
    all_gather x1, waiting for transfers between devices, local(): lax.all_gather(left, 'col', axis=1, tiled=True)  114 us
    all_gather x1, waiting for transfers between devices, local(): layer_right = lax.all_gather(right, 'row', axis=0, tiled=True)  96.1 us
    unnamed x4, waiting for transfers between devices  72.4 us
    dot_general x1, matrix products, local(): jnp.einsum('rkab,kcbe->rcae', lax.all_gather(left, 'col', axis=1, tiled=T...  31.1 us
  transfers between devices with their start and end apart: 3, of which 3 were waited for; matrix products, arithmetic and copies ran while one was open for 1% of the time, Pallas kernels for 0%

commit v1 on v0

--- a/solution.py
+++ b/solution.py
@@ -7,7 +7,23 @@
 def local(a_blocks, a_pattern, b_blocks, b_pattern, c_pattern):
     left = a_blocks * a_pattern[:, :, None, None].astype(jnp.float32)
     right = b_blocks * b_pattern[:, :, None, None].astype(jnp.float32)
-    layer_right = lax.all_gather(right, "row", axis=0, tiled=True)
+    peers, index, width = (lax.axis_size("row"), lax.axis_index("row"), right.shape[0])
+    route = [(i, (i + 1) % peers) for i in range(peers)]
+    backward = [(i, (i - 1) % peers) for i in range(peers)]
+    layer_right = jnp.zeros((*right.shape[:0], peers * width, *right.shape[0 + 1 :]), right.dtype)
+    layer_right = lax.dynamic_update_slice_in_dim(layer_right, right, index * width, axis=0)
+    from_left = from_right = right
+    halfway = peers // 2
+    for step in range(1, halfway + 1):
+        from_left = lax.ppermute(from_left, "row", route)
+        layer_right = lax.dynamic_update_slice_in_dim(
+            layer_right, from_left, (index - step) % peers * width, axis=0
+        )
+        if step < peers - halfway:
+            from_right = lax.ppermute(from_right, "row", backward)
+            layer_right = lax.dynamic_update_slice_in_dim(
+                layer_right, from_right, (index + step) % peers * width, axis=0
+            )
     partial_value = jnp.einsum(
         "rkab,kcbe->rcae",
         lax.all_gather(left, "col", axis=1, tiled=True),

time: 338 us -> 276 us (0.82)
  waiting for transfers between devices: 283 us -> 130 us
  local copies, waits for them, and re-layouts: 3.46 us -> 48.6 us
  starting transfers between devices: 0.09 us -> 44.5 us
    all_gather x1, waiting for transfers between devices: 114 us -> 0.01 us  [local(): lax.all_gather(left, 'col', axis=1, tiled=True)]
    all_gather x1 -> x0, waiting for transfers between devices: 96.1 us -> none  [local(): layer_right = lax.all_gather(right, 'row', axis=0, tiled=True)]
    ppermute x0 -> x15, waiting for transfers between devices: none -> 52.3 us  [the longest x8 47.5 us: local(): from_left = lax.ppermute(from_left, 'row', route)]
    ppermute x0 -> x15, starting transfers between devices: none -> 44.4 us  [the longest x7 26.4 us: local(): from_right = lax.ppermute(from_right, 'row', backward)]
    ppermute x0 -> x15, local copies, waits for them, and re-layouts: none -> 22.2 us  [the longest x8 11.2 us: local(): from_left = lax.ppermute(from_left, 'row', route)]
    dynamic_update_slice x0 -> x16, local copies, waits for them, and re-layouts: none -> 16.3 us  [the longest x8 8.2 us: local(): lax.dynamic_update_slice_in_dim(layer_right, from_left, (index - step) %...]
    broadcast_in_dim x0 -> x1, local copies, waits for them, and re-layouts: none -> 7.79 us  [local(): jnp.zeros((*right.shape[:0], peers * width, *right.shape[0 + 1:]), right....]
    unnamed x4 -> x3, waiting for transfers between devices: 72.4 us -> 77.3 us
  transfers between devices with their start and end apart: 3 -> 17, of which waited for: 3 -> 12; matrix products, arithmetic and copies ran while one was open for 1% -> 18% of each run, Pallas kernels for 0% -> 0%
where the time goes in v1:
time: 276 us; the launch traced here: 275 us
  waiting for transfers between devices  130 us (47%)
  local copies, waits for them, and re-layouts  48.6 us (18%)
  starting transfers between devices  44.5 us (16%)
  matrix products  31.3 us (11%)
  between operations  13.9 us (5%)
  other arithmetic  7.1 us (3%)
    unnamed x3, waiting for transfers between devices  77.3 us
    ppermute x8, waiting for transfers between devices, local(): from_left = lax.ppermute(from_left, 'row', route)  47.5 us
    dot_general x1, matrix products, local(): jnp.einsum('rkab,kcbe->rcae', lax.all_gather(left, 'col', axis=1, tiled=T...  31.3 us
    ppermute x7, starting transfers between devices, local(): from_right = lax.ppermute(from_right, 'row', backward)  26.4 us
    ppermute x8, starting transfers between devices, local(): from_left = lax.ppermute(from_left, 'row', route)  18 us
    ppermute x8, local copies, waits for them, and re-layouts, local(): from_left = lax.ppermute(from_left, 'row', route)  11.2 us
    ppermute x7, local copies, waits for them, and re-layouts, local(): from_right = lax.ppermute(from_right, 'row', backward)  11 us
    dynamic_update_slice x8, local copies, waits for them, and re-layouts, local(): lax.dynamic_update_slice_in_dim(layer_right, from_left, (index - step) %...  8.2 us
  transfers between devices with their start and end apart: 17, of which 12 were waited for; matrix products, arithmetic and copies ran while one was open for 18% of the time, Pallas kernels for 0%

profile of v1, /device:TPU:1, one launch (start us, length us, event | category | flops | bytes accessed | tf_op | source)
XLA Modules:
  0.0 274.9 jit_solution(13892822796453354971)
XLA Ops:
  7.2 2.3 broadcast_multiply_fusion
  11.7 3.0 %collective-permute-start = (f32[1,4,256,256]{3,2,1,0:T(8,128)S(1)}, f32[1,4,256,256]{3,2,1,0:T(8,128)S(1)}, u32[]{:S(2)}, u32[]{:S(2)}) collective-permute-start(f32[1,4,256,256]{3,2,1,0:T(8,128)S(1)} %broadcast_multiply_fusion.1), channel_id=1, source_target_pairs={{0,16},{16,32},{32,48},{48,64},{64,80},{80,96},{96,112},{112,128},... | collective-permute-start | bytes 3145736 | tf_op jit(solution)/shard_map/ppermute | solution.py:18
  15.0 11.5 %collective-permute-done = f32[1,4,256,256]{3,2,1,0:T(8,128)S(1)} collective-permute-done((f32[1,4,256,256]{3,2,1,0:T(8,128)S(1)}, f32[1,4,256,256]{3,2,1,0:T(8,128)S(1)}, u32[]{:S(2)}, u32[]{:S(2)}) %collective-permute-start) | collective-permute-done | bytes 1048608 | tf_op jit(solution)/shard_map/ppermute | solution.py:18
  26.5 2.5 collective-permute-start.2
  29.2 1.8 collective-permute-start.3
  31.0 9.7 %collective-permute-done.2 = f32[1,4,256,256]{3,2,1,0:T(8,128)S(1)} collective-permute-done((f32[1,4,256,256]{3,2,1,0:T(8,128)S(1)}, f32[1,4,256,256]{3,2,1,0:T(8,128)S(1)}, u32[]{:S(2)}, u32[]{:S(2)}) %collective-permute-start.2) | collective-permute-done | bytes 1048608 | tf_op jit(solution)/shard_map/ppermute | solution.py:18
  40.7 2.5 collective-permute-start.4
  43.8 2.7 collective-permute-start.5
  46.5 8.5 %collective-permute-done.4 = f32[1,4,256,256]{3,2,1,0:T(8,128)S(1)} collective-permute-done((f32[1,4,256,256]{3,2,1,0:T(8,128)S(1)}, f32[1,4,256,256]{3,2,1,0:T(8,128)S(1)}, u32[]{:S(2)}, u32[]{:S(2)}) %collective-permute-start.4) | collective-permute-done | bytes 1048608 | tf_op jit(solution)/shard_map/ppermute | solution.py:18
  54.9 2.5 collective-permute-start.6
  58.3 3.6 %collective-permute-start.7 = (f32[1,4,256,256]{3,2,1,0:T(8,128)S(1)}, f32[1,4,256,256]{3,2,1,0:T(8,128)S(1)}, u32[]{:S(2)}, u32[]{:S(2)}) collective-permute-start(f32[1,4,256,256]{3,2,1,0:T(8,128)S(1)} %collective-permute-done.5), channel_id=1, source_target_pairs={{0,240},{16,0},{32,16},{48,32},{64,48},{80,64},{96,80},{112,96},{1... | collective-permute-start | bytes 3145736 | tf_op jit(solution)/shard_map/ppermute | solution.py:23
  61.9 7.2 %collective-permute-done.6 = f32[1,4,256,256]{3,2,1,0:T(8,128)S(1)} collective-permute-done((f32[1,4,256,256]{3,2,1,0:T(8,128)S(1)}, f32[1,4,256,256]{3,2,1,0:T(8,128)S(1)}, u32[]{:S(2)}, u32[]{:S(2)}) %collective-permute-start.6) | collective-permute-done | bytes 1048608 | tf_op jit(solution)/shard_map/ppermute | solution.py:18
  69.2 2.5 collective-permute-start.8
  72.9 4.4 %collective-permute-start.9 = (f32[1,4,256,256]{3,2,1,0:T(8,128)S(1)}, f32[1,4,256,256]{3,2,1,0:T(8,128)}, u32[]{:S(2)}, u32[]{:S(2)}) collective-permute-start(f32[1,4,256,256]{3,2,1,0:T(8,128)S(1)} %collective-permute-done.7), channel_id=1, source_target_pairs={{0,240},{16,0},{32,16},{48,32},{64,48},{80,64},{96,80},{112,96},{1... | collective-permute-start | bytes 3145736 | tf_op jit(solution)/shard_map/ppermute | solution.py:23
  77.3 6.0 %collective-permute-done.8 = f32[1,4,256,256]{3,2,1,0:T(8,128)S(1)} collective-permute-done((f32[1,4,256,256]{3,2,1,0:T(8,128)S(1)}, f32[1,4,256,256]{3,2,1,0:T(8,128)S(1)}, u32[]{:S(2)}, u32[]{:S(2)}) %collective-permute-start.8) | collective-permute-done | bytes 1048608 | tf_op jit(solution)/shard_map/ppermute | solution.py:18
  83.4 2.5 collective-permute-start.10
  87.5 5.5 %collective-permute-start.11 = (f32[1,4,256,256]{3,2,1,0:T(8,128)}, f32[1,4,256,256]{3,2,1,0:T(8,128)}, u32[]{:S(2)}, u32[]{:S(2)}) collective-permute-start(f32[1,4,256,256]{3,2,1,0:T(8,128)} %collective-permute-done.9), channel_id=1, source_target_pairs={{0,240},{16,0},{32,16},{48,32},{64,48},{80,64},{96,80},{112,96},{1... | collective-permute-start | bytes 3145736 | tf_op jit(solution)/shard_map/ppermute | solution.py:23
  93.0 4.6 %collective-permute-done.10 = f32[1,4,256,256]{3,2,1,0:T(8,128)} collective-permute-done((f32[1,4,256,256]{3,2,1,0:T(8,128)S(1)}, f32[1,4,256,256]{3,2,1,0:T(8,128)}, u32[]{:S(2)}, u32[]{:S(2)}) %collective-permute-start.10) | collective-permute-done | bytes 1048608 | tf_op jit(solution)/shard_map/ppermute | solution.py:18
  97.6 2.6 collective-permute-start.12
  100.8 7.8 %broadcast_in_dim.2 = f32[16,4,256,256]{2,3,0,1:T(8,128)} broadcast(f32[]{:T(128)} %constant.87.clone.1), dimensions={} | broadcast | bytes 16777220 | tf_op jit(solution)/shard_map/broadcast_in_dim | solution.py:13
  123.2 8.2 %collective-permute-start.13 = (f32[1,4,256,256]{3,2,1,0:T(8,128)}, f32[1,4,256,256]{3,2,1,0:T(8,128)}, u32[]{:S(2)}, u32[]{:S(2)}) collective-permute-start(f32[1,4,256,256]{3,2,1,0:T(8,128)} %collective-permute-done.11), channel_id=1, source_target_pairs={{0,240},{16,0},{32,16},{48,32},{64,48},{80,64},{96,80},{112,96},{1... | collective-permute-start | bytes 3145736 | tf_op jit(solution)/shard_map/ppermute | solution.py:23
  155.5 31.3 %fusion.3 = f32[2,4,256,256]{2,3,0,1:T(8,128)} fusion(f32[2,16,256,256]{3,2,1,0:T(8,128)} %all-gather.2.cloned.1.call-done, f32[16,4,256,256]{2,3,0,1:T(8,128)} %constant_dynamic-update-slice_fusion), kind=kOutput, calls=%fused_computation.3 | convolution fusion | flops 25769803776 | bytes 27262976 | tf_op jit(solution)/shard_map/rkab,kcbe->rcae/dot_general | solution.py:27
  187.5 77.2 %all-reduce.3.cloned.1.call-done = f32[2,4,256,256]{2,3,0,1:T(8,128)} async-done(((f32[2,4,256,256]{2,3,0,1:T(8,128)}), f32[2,4,256,256]{2,3,0,1:T(8,128)}) %all-reduce.3.cloned.1.call-update) | async-done | bytes 2097168
  264.7 2.0 dynamic-slice_multiply_fusion
  (76 shorter events, 48.6 us)
Async XLA Ops:
  6.5 149.0 %all-gather.2.cloned.1.call-start = ((), (), s32[]{:S(2)}) async-start(), calls=%async_computation | async-start | bytes 9437184 | tf_op jit(solution)/shard_map/all_gather | solution.py:29
  9.6 255.1 %all-reduce.3.cloned.1.call-start = ((), (), s32[]{:S(2)}) async-start(), calls=%async_computation.1 | async-start | bytes 4194304
  11.7 14.8 %collective-permute-start = (f32[1,4,256,256]{3,2,1,0:T(8,128)S(1)}, f32[1,4,256,256]{3,2,1,0:T(8,128)S(1)}, u32[]{:S(2)}, u32[]{:S(2)}) collective-permute-start(f32[1,4,256,256]{3,2,1,0:T(8,128)S(1)} %broadcast_multiply_fusion.1), channel_id=1, source_target_pairs={{0,16},{16,32},{32,48},{48,64},{64,80},{80,96},{96,112},{112,128},... | collective-permute-start | bytes 3145736 | tf_op jit(solution)/shard_map/ppermute | solution.py:18
  14.7 14.5 %collective-permute-start.1 = (f32[1,4,256,256]{3,2,1,0:T(8,128)S(1)}, f32[1,4,256,256]{3,2,1,0:T(8,128)S(1)}, u32[]{:S(2)}, u32[]{:S(2)}) collective-permute-start(f32[1,4,256,256]{3,2,1,0:T(8,128)S(1)} %broadcast_multiply_fusion.1), channel_id=1, source_target_pairs={{0,240},{16,0},{32,16},{48,32},{64,48},{80,64},{96,80},{112,96},{1... | collective-permute-start | bytes 3145736 | tf_op jit(solution)/shard_map/ppermute | solution.py:23
  26.5 14.2 %collective-permute-start.2 = (f32[1,4,256,256]{3,2,1,0:T(8,128)S(1)}, f32[1,4,256,256]{3,2,1,0:T(8,128)S(1)}, u32[]{:S(2)}, u32[]{:S(2)}) collective-permute-start(f32[1,4,256,256]{3,2,1,0:T(8,128)S(1)} %collective-permute-done), channel_id=1, source_target_pairs={{0,16},{16,32},{32,48},{48,64},{64,80},{80,96},{96,112},{112,128},... | collective-permute-start | bytes 3145736 | tf_op jit(solution)/shard_map/ppermute | solution.py:18
  29.2 28.2 %copy-start.6 = (f32[1,4,256,256]{3,2,1,0:T(8,128)}, f32[1,4,256,256]{3,2,1,0:T(8,128)S(1)}, u32[]{:S(2)}) copy-start(f32[1,4,256,256]{3,2,1,0:T(8,128)S(1)} %collective-permute-done.1) | copy-start | bytes 3145732
  29.2 14.5 %collective-permute-start.3 = (f32[1,4,256,256]{3,2,1,0:T(8,128)S(1)}, f32[1,4,256,256]{3,2,1,0:T(8,128)S(1)}, u32[]{:S(2)}, u32[]{:S(2)}) collective-permute-start(f32[1,4,256,256]{3,2,1,0:T(8,128)S(1)} %collective-permute-done.1), channel_id=1, source_target_pairs={{0,240},{16,0},{32,16},{48,32},{64,48},{80,64},{96,80},{112,96},{1... | collective-permute-start | bytes 3145736 | tf_op jit(solution)/shard_map/ppermute | solution.py:23
  40.7 14.2 %collective-permute-start.4 = (f32[1,4,256,256]{3,2,1,0:T(8,128)S(1)}, f32[1,4,256,256]{3,2,1,0:T(8,128)S(1)}, u32[]{:S(2)}, u32[]{:S(2)}) collective-permute-start(f32[1,4,256,256]{3,2,1,0:T(8,128)S(1)} %collective-permute-done.2), channel_id=1, source_target_pairs={{0,16},{16,32},{32,48},{48,64},{64,80},{80,96},{96,112},{112,128},... | collective-permute-start | bytes 3145736 | tf_op jit(solution)/shard_map/ppermute | solution.py:18
  43.8 56.4 %copy-start.7 = (f32[1,4,256,256]{3,2,1,0:T(8,128)}, f32[1,4,256,256]{3,2,1,0:T(8,128)S(1)}, u32[]{:S(2)}) copy-start(f32[1,4,256,256]{3,2,1,0:T(8,128)S(1)} %collective-permute-done.3) | copy-start | bytes 3145732
  43.8 14.5 %collective-permute-start.5 = (f32[1,4,256,256]{3,2,1,0:T(8,128)S(1)}, f32[1,4,256,256]{3,2,1,0:T(8,128)S(1)}, u32[]{:S(2)}, u32[]{:S(2)}) collective-permute-start(f32[1,4,256,256]{3,2,1,0:T(8,128)S(1)} %collective-permute-done.3), channel_id=1, source_target_pairs={{0,240},{16,0},{32,16},{48,32},{64,48},{80,64},{96,80},{112,96},{1... | collective-permute-start | bytes 3145736 | tf_op jit(solution)/shard_map/ppermute | solution.py:23
  54.9 42.7 %copy-start.4 = (f32[1,4,256,256]{3,2,1,0:T(8,128)}, f32[1,4,256,256]{3,2,1,0:T(8,128)S(1)}, u32[]{:S(2)}) copy-start(f32[1,4,256,256]{3,2,1,0:T(8,128)S(1)} %collective-permute-done.4) | copy-start | bytes 3145732
  54.9 14.2 %collective-permute-start.6 = (f32[1,4,256,256]{3,2,1,0:T(8,128)S(1)}, f32[1,4,256,256]{3,2,1,0:T(8,128)S(1)}, u32[]{:S(2)}, u32[]{:S(2)}) collective-permute-start(f32[1,4,256,256]{3,2,1,0:T(8,128)S(1)} %collective-permute-done.4), channel_id=1, source_target_pairs={{0,16},{16,32},{32,48},{48,64},{64,80},{80,96},{96,112},{112,128},... | collective-permute-start | bytes 3145736 | tf_op jit(solution)/shard_map/ppermute | solution.py:18
  58.3 41.9 %copy-start.8 = (f32[1,4,256,256]{3,2,1,0:T(8,128)}, f32[1,4,256,256]{3,2,1,0:T(8,128)S(1)}, u32[]{:S(2)}) copy-start(f32[1,4,256,256]{3,2,1,0:T(8,128)S(1)} %collective-permute-done.5) | copy-start | bytes 3145732
  58.3 14.6 %collective-permute-start.7 = (f32[1,4,256,256]{3,2,1,0:T(8,128)S(1)}, f32[1,4,256,256]{3,2,1,0:T(8,128)S(1)}, u32[]{:S(2)}, u32[]{:S(2)}) collective-permute-start(f32[1,4,256,256]{3,2,1,0:T(8,128)S(1)} %collective-permute-done.5), channel_id=1, source_target_pairs={{0,240},{16,0},{32,16},{48,32},{64,48},{80,64},{96,80},{112,96},{1... | collective-permute-start | bytes 3145736 | tf_op jit(solution)/shard_map/ppermute | solution.py:23
  69.2 31.1 %copy-start.1 = (f32[1,4,256,256]{3,2,1,0:T(8,128)}, f32[1,4,256,256]{3,2,1,0:T(8,128)S(1)}, u32[]{:S(2)}) copy-start(f32[1,4,256,256]{3,2,1,0:T(8,128)S(1)} %collective-permute-done.6) | copy-start | bytes 3145732
  69.2 14.2 %collective-permute-start.8 = (f32[1,4,256,256]{3,2,1,0:T(8,128)S(1)}, f32[1,4,256,256]{3,2,1,0:T(8,128)S(1)}, u32[]{:S(2)}, u32[]{:S(2)}) collective-permute-start(f32[1,4,256,256]{3,2,1,0:T(8,128)S(1)} %collective-permute-done.6), channel_id=1, source_target_pairs={{0,16},{16,32},{32,48},{48,64},{64,80},{80,96},{96,112},{112,128},... | collective-permute-start | bytes 3145736 | tf_op jit(solution)/shard_map/ppermute | solution.py:18
  72.9 14.6 %collective-permute-start.9 = (f32[1,4,256,256]{3,2,1,0:T(8,128)S(1)}, f32[1,4,256,256]{3,2,1,0:T(8,128)}, u32[]{:S(2)}, u32[]{:S(2)}) collective-permute-start(f32[1,4,256,256]{3,2,1,0:T(8,128)S(1)} %collective-permute-done.7), channel_id=1, source_target_pairs={{0,240},{16,0},{32,16},{48,32},{64,48},{80,64},{96,80},{112,96},{1... | collective-permute-start | bytes 3145736 | tf_op jit(solution)/shard_map/ppermute | solution.py:23
  83.4 14.2 %collective-permute-start.10 = (f32[1,4,256,256]{3,2,1,0:T(8,128)S(1)}, f32[1,4,256,256]{3,2,1,0:T(8,128)}, u32[]{:S(2)}, u32[]{:S(2)}) collective-permute-start(f32[1,4,256,256]{3,2,1,0:T(8,128)S(1)} %collective-permute-done.8), channel_id=1, source_target_pairs={{0,16},{16,32},{32,48},{48,64},{64,80},{80,96},{96,112},{112,128},... | collective-permute-start | bytes 3145736 | tf_op jit(solution)/shard_map/ppermute | solution.py:18
  87.5 35.7 %collective-permute-start.11 = (f32[1,4,256,256]{3,2,1,0:T(8,128)}, f32[1,4,256,256]{3,2,1,0:T(8,128)}, u32[]{:S(2)}, u32[]{:S(2)}) collective-permute-start(f32[1,4,256,256]{3,2,1,0:T(8,128)} %collective-permute-done.9), channel_id=1, source_target_pairs={{0,240},{16,0},{32,16},{48,32},{64,48},{80,64},{96,80},{112,96},{1... | collective-permute-start | bytes 3145736 | tf_op jit(solution)/shard_map/ppermute | solution.py:23
  97.6 39.0 %collective-permute-start.12 = (f32[1,4,256,256]{3,2,1,0:T(8,128)}, f32[1,4,256,256]{3,2,1,0:T(8,128)S(1)}, u32[]{:S(2)}, u32[]{:S(2)}) collective-permute-start(f32[1,4,256,256]{3,2,1,0:T(8,128)} %collective-permute-done.10), channel_id=1, source_target_pairs={{0,16},{16,32},{32,48},{48,64},{64,80},{80,96},{96,112},{112,128},... | collective-permute-start | bytes 3145736 | tf_op jit(solution)/shard_map/ppermute | solution.py:18
  123.2 26.1 %collective-permute-start.13 = (f32[1,4,256,256]{3,2,1,0:T(8,128)}, f32[1,4,256,256]{3,2,1,0:T(8,128)}, u32[]{:S(2)}, u32[]{:S(2)}) collective-permute-start(f32[1,4,256,256]{3,2,1,0:T(8,128)} %collective-permute-done.11), channel_id=1, source_target_pairs={{0,240},{16,0},{32,16},{48,32},{64,48},{80,64},{96,80},{112,96},{1... | collective-permute-start | bytes 3145736 | tf_op jit(solution)/shard_map/ppermute | solution.py:23
  136.6 16.3 %collective-permute-start.14 = (f32[1,4,256,256]{3,2,1,0:T(8,128)S(1)}, f32[1,4,256,256]{3,2,1,0:T(8,128)}, u32[]{:S(2)}, u32[]{:S(2)}) collective-permute-start(f32[1,4,256,256]{3,2,1,0:T(8,128)S(1)} %collective-permute-done.12), channel_id=1, source_target_pairs={{0,16},{16,32},{32,48},{48,64},{64,80},{80,96},{96,112},{112,128},... | collective-permute-start | bytes 3145736 | tf_op jit(solution)/shard_map/ppermute | solution.py:18
  155.5 31.4 %copy-start.10 = (u32[256]{0:T(256)S(1)}, u32[256]{0:T(256)}, u32[]{:S(2)}) copy-start(u32[256]{0:T(256)} %constant.115) | copy-start | bytes 3076
  155.5 32.0 %copy-start.9 = (s32[1,4]{1,0:T(1,128)S(1)}, s32[1,4]{1,0:T(1,128)}, u32[]{:S(2)}) copy-start(s32[1,4]{1,0:T(1,128)} %param.9) | copy-start | bytes 52
  (4 other events, 78.1 us)
Sparse Core Ops, SparseCore 0:
  10.0 117.3 all-gather.1
  187.0 77.6 all-reduce.2
